TPU v7x, 512 devices: a whole 4x8x8 slice. The times are simulated.
512 devices in a mesh: ctx: 32 (over x, y), head: 16 (over z, core).
Axes of the slice: x: 4, y: 8, z: 8, core: 2. Of those that a mesh axis runs over, the one named last changes fastest.
Arguments:
- queries: bfloat16 [8192, 4096], P('ctx', 'head'), may hold values from -6 to 6
- keys_values: bfloat16 [8192, 1024], P('ctx'), may hold values from -6 to 6
- grad_rows: bfloat16 [8192, 2880], P('ctx', 'head'), may hold values from -6 to 6
- doc_ids: int32 [8192], replicated, may hold values from 0 to 7, never falling along the last dimension, each value on 1 to 2048 neighbouring positions
- tile_list: int32 [64], replicated, may hold values from 0 to 63, each once
Outputs:
- attended: float32 [8192, 4096], P('ctx', 'head')
- weight_grad: float32 [2880, 4096], P('ctx', 'head')
Inputs may be any that keep to these rules, and one draw needn't show every extreme that they name: `tile_list`: every slot index names a different tile. `doc_ids`: never falling along the window; each document holds 1 to 2048 positions.
All inputs are finite; a program needn't handle non-finite values.
Results may differ from a plain program's by a relative error of at most 0.0018.
Values may be sent and summed in bfloat16 or wider, within the bound.
No kernel may reach another device: no remote copies, remote signals or barrier semaphores. Data moves between devices by JAX's collectives and lax.ppermute only.
A program may use at most 128 MiB of HBM per device.

v0:
```python
import jax
import jax.numpy as jnp
from jax import lax
from jax.sharding import PartitionSpec as P

H = 64
KVH = 8
DH = 64
TILE = 128
NEG_FILL = -1e30


def on_device(queries, keys_values, grad_rows, doc_ids, tile_list):
    tokens_local = queries.shape[0]
    heads_local = queries.shape[1] // DH
    group = H // KVH
    kv_local = max(1, heads_local // group)
    per_kv = heads_local // kv_local
    scale = DH ** (-0.5)
    head_index = lax.axis_index("head")
    kv_start = head_index * heads_local // group
    own_kv = lax.dynamic_slice_in_dim(keys_values, kv_start * 2 * DH, kv_local * 2 * DH, 1)
    tile_count = tile_list.shape[0]
    offsets = jnp.arange(TILE, dtype=jnp.int32)
    slot_pos = (tile_list[:, None] * TILE + offsets[None, :]).reshape(-1)
    slot_doc = doc_ids.reshape(tile_count, TILE)[tile_list].reshape(-1)
    row_start = lax.axis_index("ctx") * tokens_local
    query_pos = lax.dynamic_slice_in_dim(slot_pos, row_start, tokens_local)
    query_doc = lax.dynamic_slice_in_dim(slot_doc, row_start, tokens_local)
    grouped = queries.reshape(tokens_local, kv_local, per_kv, DH)
    piece = lax.all_gather(own_kv, "ctx", axis=0, tiled=True)
    count = piece.shape[0]
    allowed = (query_doc[:, None] == slot_doc[None, :]) & (slot_pos[None, :] <= query_pos[:, None])
    run_max = jnp.full((kv_local, per_kv, tokens_local), NEG_FILL, jnp.float32)
    parts = piece.reshape(count, kv_local, 2, DH)
    keys = parts[:, :, 0]
    values = parts[:, :, 1]
    scores = jnp.einsum("tgqd,ngd->gqtn", grouped, keys, preferred_element_type=jnp.float32) * scale
    masked = jnp.where(allowed, scores, NEG_FILL)
    new_max = jnp.maximum(run_max, jnp.max(masked, axis=-1))
    weights = jnp.where(allowed, jnp.exp(masked - new_max[..., None]), 0.0)
    new_sum = jnp.sum(weights, axis=-1)
    added = jnp.einsum(
        "gqtn,ngd->gqtd", weights.astype(jnp.bfloat16), values, preferred_element_type=jnp.float32
    )
    normed = added / new_sum[..., None]
    attended = jnp.transpose(normed, (2, 0, 1, 3)).reshape(tokens_local, heads_local * DH)
    term = lax.dot_general(
        lax.all_gather(grad_rows, "head", axis=1, tiled=True).astype(jnp.float32),
        attended,
        (((0,), (0,)), ((), ())),
        precision=lax.Precision.HIGHEST,
        preferred_element_type=jnp.float32,
    )
    summed = lax.psum(term, "ctx")
    share = summed.shape[0] // lax.axis_size("ctx")
    weight_grad = lax.dynamic_slice_in_dim(summed, lax.axis_index("ctx") * share, share, 0)
    return (attended, weight_grad)


def solution(mesh):
    in_specs = (P("ctx", "head"), P("ctx", None), P("ctx", "head"), P(), P())
    out_specs = (P("ctx", "head"), P("ctx", "head"))
    return jax.shard_map(
        on_device, mesh=mesh, in_specs=in_specs, out_specs=out_specs, check_vma=False
    )
```

profile of v0, /device:TPU:16, one launch (start us, length us, event | category | flops | bytes accessed | tf_op | source)
XLA Modules:
  0.0 366.6 jit_solution(1659560030699857460)
XLA Ops:
  7.2 0.0 copy-start
  7.2 0.0 all-gather.6.cloned.1.call-start
  7.2 0.7 all-gather.6.cloned.1.call-update
  7.9 0.0 all-gather.4.cloned.1.call-start
  8.0 0.2 copy-done
  8.2 0.6 constant_dynamic-slice_fusion.1
  8.9 0.0 all-gather.4.cloned.1.call-update
  8.9 0.0 all-reduce.2.cloned.1.call-start
  8.9 0.7 compare_select_fusion
  9.6 1.4 gather_fusion
  11.0 0.1 dynamic_slice.12
  11.0 0.1 add_bitcast_fusion
  11.1 0.1 dynamic_slice.13
  11.2 1.0 copy.16
  12.2 5.7 %compare_and_fusion = pred[256,8192]{0,1:T(8,128)(4,1)S(1)} fusion(s32[256]{0:T(256)S(1)} %dynamic_slice.13, s32[256]{0:T(256)S(1)} %dynamic_slice.12, s32[8192]{0:T(1024)S(1)} %add_bitcast_fusion, s32[8192]{0:T(1024)S(1)} %bitcast.59), kind=kLoop, calls=%fused_computation.9 | loop fusion | flops 6291456 | bytes 2164736 | tf_op jit(solution)/shard_map/and | solution.py:33
  17.9 39.0 %all-gather.6.cloned.1.call-done = bf16[16,180,256]{2,1,0:T(8,128)(2,1)} async-done(((bf16[1,180,256]{2,1,0:T(8,128)(2,1)}), bf16[16,180,256]{2,1,0:T(8,128)(2,1)}) %all-gather.6.cloned.1.call-update) | async-done | bytes 1474576 | tf_op jit(solution)/shard_map/all_gather | solution.py:49
  56.9 3.3 reshape.91
  60.2 81.3 %all-gather.4.cloned.1.call-done = bf16[8192,128]{1,0:T(8,128)(2,1)} async-done(((bf16[256,128]{1,0:T(8,128)(2,1)}), bf16[8192,128]{1,0:T(8,128)(2,1)}) %all-gather.4.cloned.1.call-update) | async-done | bytes 2097168 | tf_op jit(solution)/shard_map/all_gather | solution.py:31
  141.4 4.1 %copy.15 = bf16[8192,128]{0,1:T(8,128)(2,1)} copy(bf16[8192,128]{1,0:T(8,128)(2,1)} %all-gather.4.cloned.1.call-done) | data formatting | bytes 4194304 | tf_op jit(solution)/shard_map/all_gather | solution.py:31
  145.5 14.5 %fusion = (f32[4,256]{1,0:T(4,128)S(1)}, f32[8192,256,4]{1,0,2:T(8,128)}) fusion(pred[256,8192]{0,1:T(8,128)(4,1)S(1)} %compare_and_fusion, bf16[256,4,64]{0,2,1:T(8,128)(2,1)S(1)} %bitcast.60, bf16[8192,1,2,64]{0,3,2,1:T(8,128)(2,1)} %bitcast.54), kind=kOutput, calls=%fused_computation.3 | convolution fusion | flops 1098906624 | bytes 36835328 | tf_op jit(solution)/shard_map/tgqd,ngd->gqtn/dot_general | solution.py:38
  160.0 15.0 %fusion.1 = f32[4,256]{1,0:T(4,128)S(1)} fusion(f32[8192,256,4]{1,0,2:T(8,128)} %get-tuple-element.11, f32[4,256]{1,0:T(4,128)S(1)} %broadcast_maximum_fusion, pred[256,8192]{0,1:T(8,128)(4,1)S(1)} %compare_and_fusion), kind=kLoop, calls=%fused_computation.4 | loop fusion | flops 41942016 | bytes 35659776 | tf_op jit(solution)/shard_map/reduce_sum | solution.py:42
  175.0 0.0 copy-start.1
  175.0 14.5 %fusion.7 = f32[4,256,64]{1,2,0:T(8,128)S(1)} fusion(f32[8192,256,4]{1,0,2:T(8,128)} %get-tuple-element.11, f32[4,256]{1,0:T(4,128)S(1)} %broadcast_maximum_fusion, pred[256,8192]{0,1:T(8,128)(4,1)S(1)} %compare_and_fusion, bf16[8192,1,2,64]{0,3,2,1:T(8,128)(2,1)} %bitcast.55, f32[4,256]{1,0:T(4,128)S(1)} %fusion.1), kind=kOutput, calls=%fused_computation.11 | convolution fusion | flops 1115750400 | bytes 36970496 | tf_op jit(solution)/shard_map/gqtn,ngd->gqtd/dot_general | solution.py:43
  189.5 0.0 copy-done.1
  189.5 3.0 convolution_bitcast_fusion
  192.5 0.0 all-reduce.2.cloned.1.call-update
  192.6 0.8 copy.18
  193.4 165.1 %all-reduce.2.cloned.1.call-done = f32[2880,256]{1,0:T(8,128)} async-done(((f32[2880,256]{1,0:T(8,128)}), f32[2880,256]{1,0:T(8,128)}) %all-reduce.2.cloned.1.call-update) | async-done | bytes 2949136 | tf_op jit(solution)/shard_map/psum | solution.py:55
  358.5 1.5 constant_dynamic-slice_fusion
  (2 shorter events, 0.0 us)
Async XLA Ops:
  7.2 1.0 copy-start
  7.2 49.7 %all-gather.6.cloned.1.call-start = ((), (), s32[]{:S(2)}) async-start(), calls=%async_computation.2 | async-start | bytes 1601536 | tf_op jit(solution)/shard_map/all_gather | solution.py:49
  7.9 133.5 %all-gather.4.cloned.1.call-start = ((), (), s32[]{:S(2)}) async-start(), calls=%async_computation | async-start | bytes 2162688 | tf_op jit(solution)/shard_map/all_gather | solution.py:31
  8.9 349.6 %all-reduce.2.cloned.1.call-start = ((), (), s32[]{:S(2)}) async-start(), calls=%async_computation.1 | async-start | bytes 5898240 | tf_op jit(solution)/shard_map/psum | solution.py:55
  175.0 14.5 %copy-start.1 = (bf16[2880,256]{1,0:T(8,128)(2,1)S(1)}, bf16[2880,256]{1,0:T(8,128)(2,1)}, u32[]{:S(2)}) copy-start(bf16[2880,256]{1,0:T(8,128)(2,1)} %reshape.91) | copy-start | bytes 4423684
Sparse Core Ops, SparseCore 0:
  10.1 46.7 all-gather.5
  60.6 80.7 all-gather.3
  192.7 165.7 all-reduce.1
where the time goes:
time: 367 us
  waiting for transfers between devices  286 us (78%)
  matrix products  32 us (9%)
  other arithmetic  21.4 us (6%)
  between operations  13.8 us (4%)
  local copies, waits for them, and re-layouts  13.2 us (4%)
    psum x1, waiting for transfers between devices, on_device(): summed = lax.psum(term, 'ctx')  165 us
    all_gather x1, waiting for transfers between devices, on_device(): piece = lax.all_gather(own_kv, 'ctx', axis=0, tiled=True)  81.3 us
    all_gather x1, waiting for transfers between devices, on_device(): lax.all_gather(grad_rows, 'head', axis=1, tiled=True).astype(jnp.float32)  39 us
    reduce_sum x1, other arithmetic, on_device(): new_sum = jnp.sum(weights, axis=-1)  15 us
    dot_general x1, matrix products, on_device(): jnp.einsum('gqtn,ngd->gqtd', weights.astype(jnp.bfloat16), values, prefer...  14.5 us
    dot_general x1, matrix products, on_device(): jnp.einsum('tgqd,ngd->gqtn', grouped, keys, preferred_element_type=jnp.fl...  14.5 us
  transfers between devices with their start and end apart: 3, of which 3 were waited for; matrix products, arithmetic and copies ran while one was open for 4% of the time, Pallas kernels for 0%

commit v1 on v0

--- a/solution.py
+++ b/solution.py
@@ -1,3 +1,4 @@
+import functools
 import jax
 import jax.numpy as jnp
 from jax import lax
@@ -8,6 +9,24 @@
 DH = 64
 TILE = 128
 NEG_FILL = -1e30
+
+
+def see_ends(piece_in, link_axis):
+    extent = lax.axis_size(link_axis)
+
+    def _clear_kinds(known, clean):
+        if clean >= extent:
+            return known
+        rack = []
+        for to_i in range(extent):
+            rack.append((to_i, to_i ^ clean))
+        reply = lax.ppermute(known, link_axis, rack)
+        return _clear_kinds(known + reply, 2 * clean)
+
+    return _clear_kinds(piece_in, 1)
+
+
+turn_rings_all = functools.partial(see_ends, link_axis="ctx")
 
 
 def on_device(queries, keys_values, grad_rows, doc_ids, tile_list):
@@ -52,7 +71,7 @@
         precision=lax.Precision.HIGHEST,
         preferred_element_type=jnp.float32,
     )
-    summed = lax.psum(term, "ctx")
+    summed = turn_rings_all(term)
     share = summed.shape[0] // lax.axis_size("ctx")
     weight_grad = lax.dynamic_slice_in_dim(summed, lax.axis_index("ctx") * share, share, 0)
     return (attended, weight_grad)

time: 367 us -> 660 us (1.80)
  the two profiles are of different devices: /device:TPU:16 before, /device:TPU:24 now
where the time goes in v1:
time: 660 us
  waiting for transfers between devices  563 us (85%)
  matrix products  30.3 us (5%)
  other arithmetic  24.5 us (4%)
  starting transfers between devices  14.7 us (2%)
  between operations  14.2 us (2%)
  local copies, waits for them, and re-layouts  12.6 us (2%)
    ppermute x5, waiting for transfers between devices, _clear_kinds(): reply = lax.ppermute(known, link_axis, rack)  443 us
    all_gather x1, waiting for transfers between devices, on_device(): piece = lax.all_gather(own_kv, 'ctx', axis=0, tiled=True)  80.5 us
    all_gather x1, waiting for transfers between devices, on_device(): lax.all_gather(grad_rows, 'head', axis=1, tiled=True).astype(jnp.float32)  39 us
    reduce_sum x1, other arithmetic, on_device(): new_sum = jnp.sum(weights, axis=-1)  15 us
    ppermute x5, starting transfers between devices, _clear_kinds(): reply = lax.ppermute(known, link_axis, rack)  14.6 us
    dot_general x1, matrix products, on_device(): jnp.einsum('gqtn,ngd->gqtd', weights.astype(jnp.bfloat16), values, prefer...  14.5 us
    dot_general x1, matrix products, on_device(): jnp.einsum('tgqd,ngd->gqtn', grouped, keys, preferred_element_type=jnp.fl...  14.5 us
  transfers between devices with their start and end apart: 7, of which 7 were waited for; matrix products, arithmetic and copies ran while one was open for 2% of the time, Pallas kernels for 0%

profile of v1, /device:TPU:24, one launch (start us, length us, event | category | flops | bytes accessed | tf_op | source)
XLA Modules:
  0.0 659.6 jit_solution(18230904816165321410)
XLA Ops:
  7.2 0.7 all-gather.6.cloned.1.call-update
  8.0 0.2 copy-done
  8.2 0.6 constant_dynamic-slice_fusion
  8.9 0.7 compare_select_fusion
  9.6 1.4 gather_fusion
  10.9 0.1 dynamic_slice.12
  11.1 1.0 copy.16
  12.2 5.7 compare_and_fusion
  17.8 39.0 %all-gather.6.cloned.1.call-done = bf16[16,180,256]{2,1,0:T(8,128)(2,1)} async-done(((bf16[1,180,256]{2,1,0:T(8,128)(2,1)}), bf16[16,180,256]{2,1,0:T(8,128)(2,1)}) %all-gather.6.cloned.1.call-update) | async-done | bytes 1474576 | tf_op jit(solution)/shard_map/all_gather | solution.py:68
  56.8 3.3 reshape.91
  60.1 80.5 %all-gather.4.cloned.1.call-done = bf16[8192,128]{1,0:T(8,128)(2,1)} async-done(((bf16[256,128]{1,0:T(8,128)(2,1)}), bf16[8192,128]{1,0:T(8,128)(2,1)}) %all-gather.4.cloned.1.call-update) | async-done | bytes 2097168 | tf_op jit(solution)/shard_map/all_gather | solution.py:50
  140.6 4.1 copy.15
  144.7 14.5 %fusion = (f32[4,256]{1,0:T(4,128)S(1)}, f32[8192,256,4]{1,0,2:T(8,128)}) fusion(pred[256,8192]{0,1:T(8,128)(4,1)S(1)} %compare_and_fusion, bf16[256,4,64]{0,2,1:T(8,128)(2,1)S(1)} %bitcast.60, bf16[8192,1,2,64]{0,3,2,1:T(8,128)(2,1)} %bitcast.54), kind=kOutput, calls=%fused_computation.3 | convolution fusion | flops 1098906624 | bytes 36835328 | tf_op jit(solution)/shard_map/tgqd,ngd->gqtn/dot_general | solution.py:57
  159.1 15.0 %fusion.1 = f32[4,256]{1,0:T(4,128)S(1)} fusion(f32[8192,256,4]{1,0,2:T(8,128)} %get-tuple-element.11, f32[4,256]{1,0:T(4,128)S(1)} %broadcast_maximum_fusion, pred[256,8192]{0,1:T(8,128)(4,1)S(1)} %compare_and_fusion), kind=kLoop, calls=%fused_computation.4 | loop fusion | flops 41942016 | bytes 35659776 | tf_op jit(solution)/shard_map/reduce_sum | solution.py:61
  174.1 14.5 %fusion.7 = f32[4,256,64]{1,2,0:T(8,128)S(1)} fusion(f32[8192,256,4]{1,0,2:T(8,128)} %get-tuple-element.11, f32[4,256]{1,0:T(4,128)S(1)} %broadcast_maximum_fusion, pred[256,8192]{0,1:T(8,128)(4,1)S(1)} %compare_and_fusion, bf16[8192,1,2,64]{0,3,2,1:T(8,128)(2,1)} %bitcast.55, f32[4,256]{1,0:T(4,128)S(1)} %fusion.1), kind=kOutput, calls=%fused_computation.11 | convolution fusion | flops 1115750400 | bytes 36970496 | tf_op jit(solution)/shard_map/gqtn,ngd->gqtd/dot_general | solution.py:62
  188.6 1.4 convolution_bitcast_fusion
  190.0 3.2 collective-permute-start
  193.2 60.1 %collective-permute-done = f32[2880,256]{1,0:T(8,128)S(1)} collective-permute-done((f32[2880,256]{1,0:T(8,128)S(1)}, f32[2880,256]{1,0:T(8,128)S(1)}, u32[]{:S(2)}, u32[]{:S(2)}) %collective-permute-start) | collective-permute-done | bytes 2949152 | tf_op jit(solution)/shard_map/ppermute | solution.py:23
  253.3 0.4 add.61
  253.7 2.8 collective-permute-start.1
  256.5 123.7 %collective-permute-done.1 = f32[2880,256]{1,0:T(8,128)S(1)} collective-permute-done((f32[2880,256]{1,0:T(8,128)S(1)}, f32[2880,256]{1,0:T(8,128)S(1)}, u32[]{:S(2)}, u32[]{:S(2)}) %collective-permute-start.1) | collective-permute-done | bytes 2949152 | tf_op jit(solution)/shard_map/ppermute | solution.py:23
  380.2 0.4 add.62
  380.6 4.7 collective-permute-start.2
  385.3 129.3 %collective-permute-done.2 = f32[2880,256]{1,0:T(8,128)S(1)} collective-permute-done((f32[2880,256]{1,0:T(8,128)S(1)}, f32[2880,256]{1,0:T(8,128)S(1)}, u32[]{:S(2)}, u32[]{:S(2)}) %collective-permute-start.2) | collective-permute-done | bytes 2949152 | tf_op jit(solution)/shard_map/ppermute | solution.py:23
  514.7 0.4 add.63
  515.0 1.9 collective-permute-start.3
  517.0 65.6 %collective-permute-done.3 = f32[2880,256]{1,0:T(8,128)S(1)} collective-permute-done((f32[2880,256]{1,0:T(8,128)S(1)}, f32[2880,256]{1,0:T(8,128)S(1)}, u32[]{:S(2)}, u32[]{:S(2)}) %collective-permute-start.3) | collective-permute-done | bytes 2949152 | tf_op jit(solution)/shard_map/ppermute | solution.py:23
  582.6 0.4 add.64
  583.0 1.9 collective-permute-start.4
  584.9 1.8 copy.18
  586.7 64.6 %collective-permute-done.4 = f32[2880,256]{1,0:T(8,128)} collective-permute-done((f32[2880,256]{1,0:T(8,128)S(1)}, f32[2880,256]{1,0:T(8,128)}, u32[]{:S(2)}, u32[]{:S(2)}) %collective-permute-start.4) | collective-permute-done | bytes 2949152 | tf_op jit(solution)/shard_map/ppermute | solution.py:23
  651.2 1.6 dynamic-slice_add_fusion
  (14 shorter events, 0.3 us)
Async XLA Ops:
  7.2 1.1 copy-start
  7.2 49.6 %all-gather.6.cloned.1.call-start = ((), (), s32[]{:S(2)}) async-start(), calls=%async_computation.1 | async-start | bytes 1601536 | tf_op jit(solution)/shard_map/all_gather | solution.py:68
  7.9 132.7 %all-gather.4.cloned.1.call-start = ((), (), s32[]{:S(2)}) async-start(), calls=%async_computation | async-start | bytes 2162688 | tf_op jit(solution)/shard_map/all_gather | solution.py:50
  174.1 14.5 %copy-start.2 = (bf16[2880,256]{1,0:T(8,128)(2,1)S(1)}, bf16[2880,256]{1,0:T(8,128)(2,1)}, u32[]{:S(2)}) copy-start(bf16[2880,256]{1,0:T(8,128)(2,1)} %reshape.91) | copy-start | bytes 4423684
  188.6 67.9 %copy-start.3 = (f32[4,256,64]{1,2,0:T(8,128)}, f32[4,256,64]{1,2,0:T(8,128)S(1)}, u32[]{:S(2)}) copy-start(f32[4,256,64]{1,2,0:T(8,128)S(1)} %fusion.7) | copy-start | bytes 786436
  190.0 63.3 %collective-permute-start = (f32[2880,256]{1,0:T(8,128)S(1)}, f32[2880,256]{1,0:T(8,128)S(1)}, u32[]{:S(2)}, u32[]{:S(2)}) collective-permute-start(f32[2880,256]{1,0:T(8,128)S(1)} %convolution_bitcast_fusion), channel_id=1, source_target_pairs={{0,16},{16,0},{32,48},{48,32},{64,80},{80,64},{96,112},{112,96},{1... | collective-permute-start | bytes 8847368 | tf_op jit(solution)/shard_map/ppermute | solution.py:23
  253.7 126.5 %collective-permute-start.1 = (f32[2880,256]{1,0:T(8,128)S(1)}, f32[2880,256]{1,0:T(8,128)S(1)}, u32[]{:S(2)}, u32[]{:S(2)}) collective-permute-start(f32[2880,256]{1,0:T(8,128)S(1)} %add.61), channel_id=1, source_target_pairs={{0,32},{16,48},{32,0},{48,16},{64,96},{80,112},{96,64},{112,80},{1... | collective-permute-start | bytes 8847368 | tf_op jit(solution)/shard_map/ppermute | solution.py:23
  380.2 272.6 %copy-start.1 = (bf16[256,1024]{1,0:T(8,128)(2,1)S(1)}, bf16[256,1024]{1,0:T(8,128)(2,1)}, u32[]{:S(2)}) copy-start(bf16[256,1024]{1,0:T(8,128)(2,1)} %param.6) | copy-start | bytes 1572868
  380.6 134.1 %collective-permute-start.2 = (f32[2880,256]{1,0:T(8,128)S(1)}, f32[2880,256]{1,0:T(8,128)S(1)}, u32[]{:S(2)}, u32[]{:S(2)}) collective-permute-start(f32[2880,256]{1,0:T(8,128)S(1)} %add.62), channel_id=1, source_target_pairs={{0,64},{16,80},{32,96},{48,112},{64,0},{80,16},{96,32},{112,48},{1... | collective-permute-start | bytes 8847368 | tf_op jit(solution)/shard_map/ppermute | solution.py:23
  515.0 67.5 %collective-permute-start.3 = (f32[2880,256]{1,0:T(8,128)S(1)}, f32[2880,256]{1,0:T(8,128)S(1)}, u32[]{:S(2)}, u32[]{:S(2)}) collective-permute-start(f32[2880,256]{1,0:T(8,128)S(1)} %add.63), channel_id=1, source_target_pairs={{0,128},{16,144},{32,160},{48,176},{64,192},{80,208},{96,224},{112... | collective-permute-start | bytes 8847368 | tf_op jit(solution)/shard_map/ppermute | solution.py:23
  583.0 68.3 %collective-permute-start.4 = (f32[2880,256]{1,0:T(8,128)S(1)}, f32[2880,256]{1,0:T(8,128)}, u32[]{:S(2)}, u32[]{:S(2)}) collective-permute-start(f32[2880,256]{1,0:T(8,128)S(1)} %add.64), channel_id=1, source_target_pairs={{0,256},{16,272},{32,288},{48,304},{64,320},{80,336},{96,352},{112... | collective-permute-start | bytes 8847368 | tf_op jit(solution)/shard_map/ppermute | solution.py:23
Sparse Core Ops, SparseCore 0:
  10.1 46.6 all-gather.5
  60.5 80.0 all-gather.3
